TPU v7x, 32 devices: a whole 2x2x4 slice. The times are simulated.
32 devices in a mesh: chain: 4 (over x, core), band: 8 (over z, y).
Axes of the slice: x: 2, y: 2, z: 4, core: 2. Of those that a mesh axis runs over, the one named last changes fastest.
Arguments:
- diag_inverse: float32 [8192, 2048], P(('chain', 'band'))
- coupling: float32 [8192, 2048], P('chain', 'band'), may hold values from -0.09375 to 0.09375
- elem_stiff: float32 [24, 24, 16384], P(None, None, ('chain', 'band')), may hold values from -6 to 6
- elem_mass: float32 [24, 24, 16384], P(None, None, ('chain', 'band')), may hold values from -6 to 6
- elem_dofs: int32 [24, 16384], P(None, ('chain', 'band')), may hold values from 0 to 2047
- elem_slab: int32 [16384, 1], P(('chain', 'band')), may hold values from 0 to 3; in each aligned block of 512 rows (0 to 511, 512 to 1023, ...) at most 256 rows name the same one
- elem_var: int32 [16384], P(('chain', 'band')), may hold values from 0 to 191
- mode: float32 [8192], P(('chain', 'band')), may hold values from -0.4 to 0.4
- mass_mode: float32 [8192], P('chain'), may hold values from -1.2 to 1.2
- eigenvalue: float32 [1], replicated, may hold values from 0.5 to 2
Outputs:
- eigvec_slope: float32 [192, 8192], P(None, ('chain', 'band'))
- eigval_slope: float32 [192], replicated
Inputs may be any that keep to these rules, and one draw needn't show every extreme that they name: `elem_slab`: within the rows of one device no slab is named by more than 256 elements, a bound that some block reaches.
All inputs are finite; a program needn't handle non-finite values.
Results may differ from a plain program's by a relative error of at most 0.00014.
Values sent between devices are 32-bit elements; how exact they have to be, the bound alone decides.
No kernel may reach another device: no remote copies, remote signals or barrier semaphores. Data moves between devices by JAX's collectives and lax.ppermute only.
A program may use at most 64 MiB of HBM per device.

v0:
```python
import jax
import jax.numpy as jnp
from jax import lax
from jax.sharding import PartitionSpec as P

VARS = 192
PANELS = 4


def from_behind(value, axis, by):
    size = lax.axis_size(axis)
    pairs = [(i, i + by) for i in range(size) if 0 <= i + by < size]
    return lax.ppermute(value, axis, pairs)


def sweep(stored, shift_by, iterations, panel_rows, piece_cols, prepare, finish):

    def advance(iteration, carry):
        outgoing, kept = carry
        received = from_behind(outgoing, "chain", shift_by)
        partial_value, context = prepare(iteration, received, kept)
        summed = lax.psum(partial_value, "band")
        return finish(iteration, summed, context, kept)

    outgoing = jnp.zeros((panel_rows, piece_cols), jnp.float32)
    return lax.fori_loop(0, iterations, advance, (outgoing, stored))[1]


def on_device(
    diag_inverse,
    coupling,
    elem_stiff,
    elem_mass,
    elem_dofs,
    elem_slab,
    elem_var,
    mode,
    mass_mode,
    eigenvalue,
):
    highest = lax.Precision.HIGHEST
    chain_len = lax.axis_size("chain")
    chain_pos = lax.axis_index("chain")
    band_pos = lax.axis_index("band")
    piece_cols = diag_inverse.shape[0]
    slab_rows = diag_inverse.shape[1]
    elem_width = elem_dofs.shape[0]
    elem_count = elem_dofs.shape[1]
    capacity = 2 * elem_count // chain_len
    eigen_val = eigenvalue[0]
    whole_mode = lax.all_gather(mode, ("chain", "band"), axis=0, tiled=True)
    dest_slab = elem_slab[:, 0]
    dof_index = dest_slab[None, :] * slab_rows + elem_dofs
    mode_at = whole_mode[dof_index]
    operator = elem_stiff - eigen_val * elem_mass
    loads = -jnp.einsum("ije,je->ie", operator, mode_at, precision=highest)
    quadratic = -jnp.sum(mode_at * loads, axis=0)
    matches = (elem_var[None, :] == jnp.arange(VARS)[:, None]).astype(jnp.float32)
    local_slope = jnp.dot(matches, quadratic, precision=highest)
    eigval_slope = lax.psum(local_slope, ("chain", "band"))
    onehot = (dest_slab[:, None] == jnp.arange(chain_len)[None, :]).astype(jnp.int32)
    slot_rank = jnp.sum((jnp.cumsum(onehot, axis=0) - 1) * onehot, axis=1)
    flat_index = elem_var[None, :] * slab_rows + elem_dofs
    send_values = (
        jnp.zeros((chain_len, elem_width, capacity), jnp.float32)
        .at[dest_slab, :, slot_rank]
        .set(loads.T)
    )
    send_index = (
        jnp.zeros((chain_len, elem_width, capacity), jnp.int32)
        .at[dest_slab, :, slot_rank]
        .set(flat_index.T)
    )
    got_values, got_index = (
        lax.all_to_all(send_values, "chain", split_axis=0, concat_axis=0, tiled=True),
        lax.all_to_all(send_index, "chain", split_axis=0, concat_axis=0, tiled=True),
    )
    assembled = (
        jnp.zeros((VARS * slab_rows,), jnp.float32)
        .at[got_index.reshape(-1)]
        .add(got_values.reshape(-1))
    )
    assembled = assembled.reshape(VARS, slab_rows)
    slope_term = eigval_slope[:, None] * mass_mode[None, :]
    panel_count = PANELS
    panel_rows = VARS // panel_count
    iterations = chain_len + panel_count - 1
    contract = (((1,), (1,)), ((), ()))

    def locate(panel_index):
        active = (panel_index >= 0) & (panel_index < panel_count)
        first_row = jnp.clip(panel_index, 0, panel_count - 1) * panel_rows
        return (active, first_row)

    def place(kept, fresh, active, first_row):
        previous = lax.dynamic_slice_in_dim(kept, first_row, panel_rows, 0)
        return lax.dynamic_update_slice_in_dim(
            kept, jnp.where(active, fresh, previous), first_row, 0
        )

    def forward_prepare(iteration, received, kept):
        active, first_row = locate(iteration - chain_pos)
        rhs_panel = lax.dynamic_slice_in_dim(assembled, first_row, panel_rows, 0)
        carried = lax.dot_general(
            received, coupling, contract, precision=highest, preferred_element_type=jnp.float32
        )
        return (rhs_panel - carried, (active, first_row))

    def forward_finish(iteration, summed, context, kept):
        active, first_row = context
        coupled = summed + lax.dynamic_slice_in_dim(slope_term, first_row, panel_rows, 0)
        fresh = lax.dot_general(
            coupled, diag_inverse, contract, precision=highest, preferred_element_type=jnp.float32
        )
        return (fresh, place(kept, fresh, active, first_row))

    forward_kept = sweep(
        jnp.zeros((VARS, piece_cols), jnp.float32),
        1,
        iterations,
        panel_rows,
        piece_cols,
        forward_prepare,
        forward_finish,
    )

    def backward_prepare(iteration, received, kept):
        active, first_row = locate(iteration - (chain_len - 1 - chain_pos))
        remain = lax.dynamic_slice_in_dim(forward_kept, first_row, panel_rows, 0) - received
        partial_value = jnp.dot(
            remain, diag_inverse, precision=highest, preferred_element_type=jnp.float32
        )
        return (partial_value, (active, first_row))

    def backward_finish(iteration, summed, context, kept):
        active, first_row = context
        own_piece = lax.dynamic_slice_in_dim(summed, band_pos * piece_cols, piece_cols, 1)
        outgoing = jnp.dot(summed, coupling, precision=highest, preferred_element_type=jnp.float32)
        return (outgoing, place(kept, own_piece, active, first_row))

    eigvec_slope = sweep(
        jnp.zeros((VARS, piece_cols), jnp.float32),
        -1,
        iterations,
        panel_rows,
        piece_cols,
        backward_prepare,
        backward_finish,
    )
    return (eigvec_slope, eigval_slope)


def solution(mesh):
    in_specs = (
        P(("chain", "band"), None),
        P("chain", "band"),
        P(None, None, ("chain", "band")),
        P(None, None, ("chain", "band")),
        P(None, ("chain", "band")),
        P(("chain", "band"), None),
        P(("chain", "band")),
        P(("chain", "band")),
        P("chain"),
        P(),
    )
    out_specs = (P(None, ("chain", "band")), P())
    return jax.shard_map(
        on_device, mesh=mesh, in_specs=in_specs, out_specs=out_specs, check_vma=False
    )
```

profile of v0, /device:TPU:0, one launch (start us, length us, event | category | flops | bytes accessed | tf_op | source)
XLA Modules:
  0.0 1582.4 jit_solution(5994299352049603090)
XLA Ops:
  8.7 70.1 %all-gather = f32[32,1,256]{2,1,0:T(1,128)S(1)} all-gather(f32[1,1,256]{2,1,0:T(1,128)} %bitcast.73), channel_id=1, replica_groups=mesh['chain'=4,'band'=8] {'chain','band'}, dimensions={0}, use_global_device_ids=true | all-gather | bytes 33792 | tf_op jit(solution)/shard_map/all_gather | solution.py:51
  78.8 68.0 %gather_fusion = f32[12288]{0:T(1024)S(1)} fusion(f32[8192]{0:T(1024)S(1)} %bitcast.59, s32[12288]{0:T(1024)S(1)} %broadcast_clamp_fusion), kind=kCustom, calls=%fused_computation | custom fusion | bytes 147456 | tf_op jit(solution)/shard_map/gather | solution.py:54
  149.9 24.8 %scatter_fusion.1 = f32[4,24,256]{1,2,0:T(8,128)S(1)} fusion(f32[4,24,256]{1,2,0:T(8,128)S(1)} %broadcast_in_dim.10, s32[512]{0:T(512)S(1)} %bitcast.60, f32[512,24]{1,0:T(8,128)S(1)} %copy.19), kind=kCustom, calls=%fused_computation.2 | custom fusion | bytes 151552 | tf_op jit(solution)/shard_map/scatter | solution.py:67
  179.5 24.8 %scatter_fusion = s32[4,24,256]{1,2,0:T(8,128)S(1)} fusion(s32[4,24,256]{1,2,0:T(8,128)S(1)} %broadcast_in_dim.9, s32[512]{0:T(512)S(1)} %bitcast.61, s32[512,24]{1,0:T(8,128)S(1)} %copy.17), kind=kCustom, calls=%fused_computation.1 | custom fusion | bytes 151552 | tf_op jit(solution)/shard_map/scatter | solution.py:72
  205.2 36.8 %psum.31 = f32[192]{0:T(256)S(1)} all-reduce(f32[192]{0:T(256)S(1)} %bitcast.74), channel_id=1, replica_groups=mesh['chain'=4,'band'=8] {'chain','band'}, use_global_device_ids=true, to_apply=%region_7.8 | all-reduce | flops 192 | bytes 1536 | tf_op jit(solution)/shard_map/psum | solution.py:60
  250.0 157.2 %scatter_custom_fusion.2 = f32[393216]{0:T(1024)} fusion(s32[24576]{0:T(1024)S(1)} %bitcast.66, f32[24576]{0:T(1024)S(1)} %bitcast.65, f32[]{:T(128)} %constant.139.clone.1), kind=kCustom, calls=%fused_computation.17 | custom fusion | flops 24576 | bytes 1572868 | tf_op jit(solution)/shard_map/scatter-add | solution.py:81
  410.0 593.5 %while.32 = (s32[]{:T(128)}, f32[48,256]{1,0:T(8,128)S(1)}, f32[192,256]{1,0:T(8,128)S(1)}, s32[]{:T(128)}, f32[192,2048]{1,0:T(8,128)}, /*index=5*/f32[2048,256...) while((s32[]{:T(128)}, f32[48,256]{1,0:T(8,128)S(1)}, ...), condition=%wide.region_10.11_spmd, body=%wide.region_8.10_spmd.sunk | while | flops 604286976 | bytes 8521536 | solution.py:26
  410.1 5.6 collective-permute-start
  420.3 74.7 %all-reduce.3.cloned.1.call-done = f32[48,2048]{1,0:T(8,128)} async-done(((f32[48,2048]{1,0:T(8,128)}), f32[48,2048]{1,0:T(8,128)}) %all-reduce.3.cloned.1.call-update) | async-done | bytes 393232 | tf_op jit(solution)/shard_map/while/body/eval_jaxpr/psum | solution.py:22
  495.1 3.8 select_dynamic-update-slice_fusion.4
  501.1 3.8 convolution_subtract_fusion.2
  505.0 74.2 %all-reduce.3.cloned.1.call-done = f32[48,2048]{1,0:T(8,128)} async-done(((f32[48,2048]{1,0:T(8,128)}), f32[48,2048]{1,0:T(8,128)}) %all-reduce.3.cloned.1.call-update) | async-done | bytes 393232 | tf_op jit(solution)/shard_map/while/body/eval_jaxpr/psum | solution.py:22
  579.2 3.8 select_dynamic-update-slice_fusion.4
  589.1 74.2 %all-reduce.3.cloned.1.call-done = f32[48,2048]{1,0:T(8,128)} async-done(((f32[48,2048]{1,0:T(8,128)}), f32[48,2048]{1,0:T(8,128)}) %all-reduce.3.cloned.1.call-update) | async-done | bytes 393232 | tf_op jit(solution)/shard_map/while/body/eval_jaxpr/psum | solution.py:22
  663.3 3.8 select_dynamic-update-slice_fusion.4
  669.4 3.8 convolution_subtract_fusion.2
  673.2 74.2 %all-reduce.3.cloned.1.call-done = f32[48,2048]{1,0:T(8,128)} async-done(((f32[48,2048]{1,0:T(8,128)}), f32[48,2048]{1,0:T(8,128)}) %all-reduce.3.cloned.1.call-update) | async-done | bytes 393232 | tf_op jit(solution)/shard_map/while/body/eval_jaxpr/psum | solution.py:22
  747.4 3.8 select_dynamic-update-slice_fusion.4
  757.3 74.2 %all-reduce.3.cloned.1.call-done = f32[48,2048]{1,0:T(8,128)} async-done(((f32[48,2048]{1,0:T(8,128)}), f32[48,2048]{1,0:T(8,128)}) %all-reduce.3.cloned.1.call-update) | async-done | bytes 393232 | tf_op jit(solution)/shard_map/while/body/eval_jaxpr/psum | solution.py:22
  831.5 3.8 select_dynamic-update-slice_fusion.4
  841.4 74.2 %all-reduce.3.cloned.1.call-done = f32[48,2048]{1,0:T(8,128)} async-done(((f32[48,2048]{1,0:T(8,128)}), f32[48,2048]{1,0:T(8,128)}) %all-reduce.3.cloned.1.call-update) | async-done | bytes 393232 | tf_op jit(solution)/shard_map/while/body/eval_jaxpr/psum | solution.py:22
  915.6 3.8 select_dynamic-update-slice_fusion.4
  925.5 74.2 %all-reduce.3.cloned.1.call-done = f32[48,2048]{1,0:T(8,128)} async-done(((f32[48,2048]{1,0:T(8,128)}), f32[48,2048]{1,0:T(8,128)}) %all-reduce.3.cloned.1.call-update) | async-done | bytes 393232 | tf_op jit(solution)/shard_map/while/body/eval_jaxpr/psum | solution.py:22
  999.7 3.8 select_dynamic-update-slice_fusion.4
  1003.6 571.6 %while.33 = (s32[]{:T(128)}, f32[48,256]{1,0:T(8,128)S(1)}, f32[192,256]{1,0:T(8,128)S(1)}, s32[]{:T(128)}, f32[192,256]{1,0:T(8,128)S(1)}, /*index=5*/f32[256,2...) while((s32[]{:T(128)}, f32[48,256]{1,0:T(8,128)S(1)}, ...), condition=%wide.region_13.14_spmd, body=%wide.region_11.13_spmd.sunk | while | flops 604102656 | bytes 7831881 | solution.py:26
  1010.5 71.8 %all-reduce.5.cloned.1.call-done = f32[48,2048]{1,0:T(8,128)} async-done(((f32[48,2048]{1,0:T(8,128)}), f32[48,2048]{1,0:T(8,128)}) %all-reduce.5.cloned.1.call-update) | async-done | bytes 393232 | tf_op jit(solution)/shard_map/while/body/eval_jaxpr/psum | solution.py:22
  1092.1 71.9 %all-reduce.5.cloned.1.call-done = f32[48,2048]{1,0:T(8,128)} async-done(((f32[48,2048]{1,0:T(8,128)}), f32[48,2048]{1,0:T(8,128)}) %all-reduce.5.cloned.1.call-update) | async-done | bytes 393232 | tf_op jit(solution)/shard_map/while/body/eval_jaxpr/psum | solution.py:22
  1173.8 71.8 %all-reduce.5.cloned.1.call-done = f32[48,2048]{1,0:T(8,128)} async-done(((f32[48,2048]{1,0:T(8,128)}), f32[48,2048]{1,0:T(8,128)}) %all-reduce.5.cloned.1.call-update) | async-done | bytes 393232 | tf_op jit(solution)/shard_map/while/body/eval_jaxpr/psum | solution.py:22
  1255.5 71.8 %all-reduce.5.cloned.1.call-done = f32[48,2048]{1,0:T(8,128)} async-done(((f32[48,2048]{1,0:T(8,128)}), f32[48,2048]{1,0:T(8,128)}) %all-reduce.5.cloned.1.call-update) | async-done | bytes 393232 | tf_op jit(solution)/shard_map/while/body/eval_jaxpr/psum | solution.py:22
  1337.1 71.8 %all-reduce.5.cloned.1.call-done = f32[48,2048]{1,0:T(8,128)} async-done(((f32[48,2048]{1,0:T(8,128)}), f32[48,2048]{1,0:T(8,128)}) %all-reduce.5.cloned.1.call-update) | async-done | bytes 393232 | tf_op jit(solution)/shard_map/while/body/eval_jaxpr/psum | solution.py:22
  1418.8 71.8 %all-reduce.5.cloned.1.call-done = f32[48,2048]{1,0:T(8,128)} async-done(((f32[48,2048]{1,0:T(8,128)}), f32[48,2048]{1,0:T(8,128)}) %all-reduce.5.cloned.1.call-update) | async-done | bytes 393232 | tf_op jit(solution)/shard_map/while/body/eval_jaxpr/psum | solution.py:22
  1500.4 71.8 %all-reduce.5.cloned.1.call-done = f32[48,2048]{1,0:T(8,128)} async-done(((f32[48,2048]{1,0:T(8,128)}), f32[48,2048]{1,0:T(8,128)}) %all-reduce.5.cloned.1.call-update) | async-done | bytes 393232 | tf_op jit(solution)/shard_map/while/body/eval_jaxpr/psum | solution.py:22
  (133 shorter events, 122.2 us)
Async XLA Ops:
  175.5 70.0 %copy-start.5 = (f32[2048]{0:T(1024)S(1)}, f32[2048]{0:T(1024)}, u32[]{:S(2)}) copy-start(f32[2048]{0:T(1024)} %param.22) | copy-start | bytes 24580
  175.5 66.4 %all-to-all-start.1 = ((f32[4,24,256]{2,1,0:T(8,128)}), f32[4,24,256]{2,1,0:T(8,128)S(1)}, u32[]{:S(2)}, u32[]{:S(2)}) async-start(f32[4,24,256]{2,1,0:T(8,128)} %copy.20), calls=%async_computation.1 | async-start | bytes 196608 | tf_op jit(solution)/shard_map/all_to_all | solution.py:75
  242.0 165.3 %copy-start.6 = (f32[192]{0:T(256)}, f32[192]{0:T(256)S(1)}, u32[]{:S(2)}) copy-start(f32[192]{0:T(256)S(1)} %psum.31) | copy-start | bytes 2308
  242.0 7.8 all-to-all-start
  410.0 85.1 %all-reduce.3.cloned.1.call-start = ((), (), s32[]{:S(2)}) async-start(), calls=%async_computation.2 | async-start | bytes 786432 | tf_op jit(solution)/shard_map/while/body/eval_jaxpr/psum | solution.py:22
  410.1 6.4 collective-permute-start
  498.9 80.2 %all-reduce.3.cloned.1.call-start = ((), (), s32[]{:S(2)}) async-start(), calls=%async_computation.2 | async-start | bytes 786432 | tf_op jit(solution)/shard_map/while/body/eval_jaxpr/psum | solution.py:22
  499.0 2.2 collective-permute-start
  583.0 80.3 %all-reduce.3.cloned.1.call-start = ((), (), s32[]{:S(2)}) async-start(), calls=%async_computation.2 | async-start | bytes 786432 | tf_op jit(solution)/shard_map/while/body/eval_jaxpr/psum | solution.py:22
  583.1 2.2 collective-permute-start
  667.2 80.2 %all-reduce.3.cloned.1.call-start = ((), (), s32[]{:S(2)}) async-start(), calls=%async_computation.2 | async-start | bytes 786432 | tf_op jit(solution)/shard_map/while/body/eval_jaxpr/psum | solution.py:22
  667.2 2.2 collective-permute-start
  751.3 80.2 %all-reduce.3.cloned.1.call-start = ((), (), s32[]{:S(2)}) async-start(), calls=%async_computation.2 | async-start | bytes 786432 | tf_op jit(solution)/shard_map/while/body/eval_jaxpr/psum | solution.py:22
  751.3 2.2 collective-permute-start
  835.4 80.2 %all-reduce.3.cloned.1.call-start = ((), (), s32[]{:S(2)}) async-start(), calls=%async_computation.2 | async-start | bytes 786432 | tf_op jit(solution)/shard_map/while/body/eval_jaxpr/psum | solution.py:22
  835.4 2.2 collective-permute-start
  919.5 80.2 %all-reduce.3.cloned.1.call-start = ((), (), s32[]{:S(2)}) async-start(), calls=%async_computation.2 | async-start | bytes 786432 | tf_op jit(solution)/shard_map/while/body/eval_jaxpr/psum | solution.py:22
  919.5 2.2 collective-permute-start
  1003.6 78.7 %all-reduce.5.cloned.1.call-start = ((), (), s32[]{:S(2)}) async-start(), calls=%async_computation.3 | async-start | bytes 786432 | tf_op jit(solution)/shard_map/while/body/eval_jaxpr/psum | solution.py:22
  1003.7 3.1 collective-permute-start.1
  1085.3 78.7 %all-reduce.5.cloned.1.call-start = ((), (), s32[]{:S(2)}) async-start(), calls=%async_computation.3 | async-start | bytes 786432 | tf_op jit(solution)/shard_map/while/body/eval_jaxpr/psum | solution.py:22
  1085.3 3.1 collective-permute-start.1
  1166.9 78.7 %all-reduce.5.cloned.1.call-start = ((), (), s32[]{:S(2)}) async-start(), calls=%async_computation.3 | async-start | bytes 786432 | tf_op jit(solution)/shard_map/while/body/eval_jaxpr/psum | solution.py:22
  1167.0 3.1 collective-permute-start.1
  1248.6 78.7 %all-reduce.5.cloned.1.call-start = ((), (), s32[]{:S(2)}) async-start(), calls=%async_computation.3 | async-start | bytes 786432 | tf_op jit(solution)/shard_map/while/body/eval_jaxpr/psum | solution.py:22
  1248.6 3.1 collective-permute-start.1
  1330.2 78.7 %all-reduce.5.cloned.1.call-start = ((), (), s32[]{:S(2)}) async-start(), calls=%async_computation.3 | async-start | bytes 786432 | tf_op jit(solution)/shard_map/while/body/eval_jaxpr/psum | solution.py:22
  1330.3 3.1 collective-permute-start.1
  1411.9 78.7 %all-reduce.5.cloned.1.call-start = ((), (), s32[]{:S(2)}) async-start(), calls=%async_computation.3 | async-start | bytes 786432 | tf_op jit(solution)/shard_map/while/body/eval_jaxpr/psum | solution.py:22
  1411.9 3.1 collective-permute-start.1
  1493.5 78.7 %all-reduce.5.cloned.1.call-start = ((), (), s32[]{:S(2)}) async-start(), calls=%async_computation.3 | async-start | bytes 786432 | tf_op jit(solution)/shard_map/while/body/eval_jaxpr/psum | solution.py:22
  1493.6 3.1 collective-permute-start.1
  (6 other events, 171.2 us)
Sparse Core Ops, SparseCore 0:
  420.4 74.5 all-reduce.2
  505.1 74.0 all-reduce.2
  589.2 74.0 all-reduce.2
  673.3 74.0 all-reduce.2
  757.4 74.0 all-reduce.2
  841.5 74.0 all-reduce.2
  925.6 74.0 all-reduce.2
  1010.6 71.6 all-reduce.4
  1092.3 71.6 all-reduce.4
  1173.9 71.6 all-reduce.4
  1255.6 71.6 all-reduce.4
  1337.2 71.6 all-reduce.4
  1418.9 71.6 all-reduce.4
  1500.5 71.6 all-reduce.4
where the time goes:
time: 1580 us
  waiting for transfers between devices  1040 us (66%)
  other arithmetic  168 us (11%)
  local copies, waits for them, and re-layouts  123 us (8%)
  blocking collectives  107 us (7%)
  matrix products  94.3 us (6%)
  starting transfers between devices  29.9 us (2%)
    psum x14, waiting for transfers between devices, advance(): summed = lax.psum(partial_value, 'band')  1020 us
    scatter-add x1, other arithmetic, on_device(): assembled = jnp.zeros((VARS * slab_rows,), jnp.float32).at[got_index.resh...  157 us
    all_gather x1, blocking collectives, on_device(): whole_mode = lax.all_gather(mode, ('chain', 'band'), axis=0, tiled=True)  70.1 us
    gather x2, local copies, waits for them, and re-layouts, on_device(): mode_at = whole_mode[dof_index]  68 us
    psum x1, blocking collectives, on_device(): eigval_slope = lax.psum(local_slope, ('chain', 'band'))  36.8 us
  transfers between devices with their start and end apart: 30, of which 29 were waited for; matrix products, arithmetic and copies ran while one was open for 2% of the time, Pallas kernels for 0%

commit v1 on v0

--- a/solution.py
+++ b/solution.py
@@ -19,7 +19,7 @@
         outgoing, kept = carry
         received = from_behind(outgoing, "chain", shift_by)
         partial_value, context = prepare(iteration, received, kept)
-        summed = lax.psum(partial_value, "band")
+        summed = jnp.sum(lax.all_gather(partial_value, "band"), axis=0)
         return finish(iteration, summed, context, kept)
 
     outgoing = jnp.zeros((panel_rows, piece_cols), jnp.float32)

time: 1580 us -> 1430 us (0.905)
  waiting for transfers between devices: 1040 us -> 875 us
  other arithmetic: 168 us -> 191 us
    psum x14 -> x0, waiting for transfers between devices: 1020 us -> none  [advance(): summed = lax.psum(partial_value, 'band')]
    all_gather x0 -> x14, waiting for transfers between devices: none -> 853 us  [advance(): summed = jnp.sum(lax.all_gather(partial_value, 'band'), axis=0)]
    reduce_sum x0 -> x14, other arithmetic: none -> 29.2 us  [advance(): summed = jnp.sum(lax.all_gather(partial_value, 'band'), axis=0)]
where the time goes in v1:
time: 1430 us
  waiting for transfers between devices  875 us (61%)
  other arithmetic  191 us (13%)
  local copies, waits for them, and re-layouts  124 us (9%)
  blocking collectives  107 us (7%)
  matrix products  86.7 us (6%)
  starting transfers between devices  29.9 us (2%)
  between operations  14.6 us (1%)
    all_gather x14, waiting for transfers between devices, advance(): summed = jnp.sum(lax.all_gather(partial_value, 'band'), axis=0)  853 us
    scatter-add x1, other arithmetic, on_device(): assembled = jnp.zeros((VARS * slab_rows,), jnp.float32).at[got_index.resh...  157 us
    all_gather x1, blocking collectives, on_device(): whole_mode = lax.all_gather(mode, ('chain', 'band'), axis=0, tiled=True)  70.1 us
    gather x2, local copies, waits for them, and re-layouts, on_device(): mode_at = whole_mode[dof_index]  68 us
    psum x1, blocking collectives, on_device(): eigval_slope = lax.psum(local_slope, ('chain', 'band'))  36.8 us
    reduce_sum x14, other arithmetic, advance(): summed = jnp.sum(lax.all_gather(partial_value, 'band'), axis=0)  29.2 us
  transfers between devices with their start and end apart: 30, of which 29 were waited for; matrix products, arithmetic and copies ran while one was open for 2% of the time, Pallas kernels for 0%

profile of v1, /device:TPU:0, one launch (start us, length us, event | category | flops | bytes accessed | tf_op | source)
XLA Modules:
  0.0 1429.3 jit_solution(11021643182220738510)
XLA Ops:
  8.7 70.1 %all-gather.2 = f32[32,1,256]{2,1,0:T(1,128)S(1)} all-gather(f32[1,1,256]{2,1,0:T(1,128)} %bitcast.81), channel_id=1, replica_groups=mesh['chain'=4,'band'=8] {'chain','band'}, dimensions={0}, use_global_device_ids=true | all-gather | bytes 33792 | tf_op jit(solution)/shard_map/all_gather | solution.py:51
  78.8 68.0 %gather_fusion = f32[12288]{0:T(1024)S(1)} fusion(f32[8192]{0:T(1024)S(1)} %bitcast.65, s32[12288]{0:T(1024)S(1)} %broadcast_clamp_fusion), kind=kCustom, calls=%fused_computation | custom fusion | bytes 147456 | tf_op jit(solution)/shard_map/gather | solution.py:54
  149.9 24.8 %scatter_fusion.1 = f32[4,24,256]{1,2,0:T(8,128)S(1)} fusion(f32[4,24,256]{1,2,0:T(8,128)S(1)} %broadcast_in_dim.10, s32[512]{0:T(512)S(1)} %bitcast.66, f32[512,24]{1,0:T(8,128)S(1)} %copy.19), kind=kCustom, calls=%fused_computation.2 | custom fusion | bytes 151552 | tf_op jit(solution)/shard_map/scatter | solution.py:67
  179.5 24.8 %scatter_fusion = s32[4,24,256]{1,2,0:T(8,128)S(1)} fusion(s32[4,24,256]{1,2,0:T(8,128)S(1)} %broadcast_in_dim.9, s32[512]{0:T(512)S(1)} %bitcast.67, s32[512,24]{1,0:T(8,128)S(1)} %copy.17), kind=kCustom, calls=%fused_computation.1 | custom fusion | bytes 151552 | tf_op jit(solution)/shard_map/scatter | solution.py:72
  205.2 36.8 %psum.7 = f32[192]{0:T(256)S(1)} all-reduce(f32[192]{0:T(256)S(1)} %bitcast.82), channel_id=1, replica_groups=mesh['chain'=4,'band'=8] {'chain','band'}, use_global_device_ids=true, to_apply=%region_7.8 | all-reduce | flops 192 | bytes 1536 | tf_op jit(solution)/shard_map/psum | solution.py:60
  250.0 157.3 %scatter_custom_fusion.2 = f32[393216]{0:T(1024)} fusion(s32[24576]{0:T(1024)S(1)} %bitcast.74, f32[24576]{0:T(1024)S(1)} %bitcast.73, f32[]{:T(128)} %constant.153.clone.1), kind=kCustom, calls=%fused_computation.17 | custom fusion | flops 24576 | bytes 1572868 | tf_op jit(solution)/shard_map/scatter-add | solution.py:81
  410.1 523.1 %while.32 = (s32[]{:T(128)}, f32[48,256]{1,0:T(8,128)S(1)}, f32[192,256]{1,0:T(8,128)S(1)}, s32[]{:T(128)}, f32[192,2048]{1,0:T(8,128)}, /*index=5*/f32[2048,256...) while((s32[]{:T(128)}, f32[48,256]{1,0:T(8,128)S(1)}, ...), condition=%wide.region_10.11_spmd, body=%wide.region_8.10_spmd.sunk | while | flops 604876800 | bytes 20318028 | solution.py:26
  410.1 5.6 collective-permute-start
  416.6 3.8 convolution_subtract_fusion.2
  420.4 63.0 %all-gather.10.cloned.1.call-done = f32[384,2048]{1,0:T(8,128)} async-done(((f32[48,2048]{1,0:T(8,128)}), f32[384,2048]{1,0:T(8,128)}) %all-gather.10.cloned.1.call-update) | async-done | bytes 3145744 | tf_op jit(solution)/shard_map/while/body/eval_jaxpr/all_gather | solution.py:22
  485.5 3.7 select_dynamic-update-slice_fusion.4
  491.5 3.8 convolution_subtract_fusion.2
  495.3 62.1 %all-gather.10.cloned.1.call-done = f32[384,2048]{1,0:T(8,128)} async-done(((f32[48,2048]{1,0:T(8,128)}), f32[384,2048]{1,0:T(8,128)}) %all-gather.10.cloned.1.call-update) | async-done | bytes 3145744 | tf_op jit(solution)/shard_map/while/body/eval_jaxpr/all_gather | solution.py:22
  565.5 3.8 convolution_subtract_fusion.2
  569.3 62.1 %all-gather.10.cloned.1.call-done = f32[384,2048]{1,0:T(8,128)} async-done(((f32[48,2048]{1,0:T(8,128)}), f32[384,2048]{1,0:T(8,128)}) %all-gather.10.cloned.1.call-update) | async-done | bytes 3145744 | tf_op jit(solution)/shard_map/while/body/eval_jaxpr/all_gather | solution.py:22
  633.5 3.7 select_dynamic-update-slice_fusion.4
  639.4 3.8 convolution_subtract_fusion.2
  643.3 62.1 %all-gather.10.cloned.1.call-done = f32[384,2048]{1,0:T(8,128)} async-done(((f32[48,2048]{1,0:T(8,128)}), f32[384,2048]{1,0:T(8,128)}) %all-gather.10.cloned.1.call-update) | async-done | bytes 3145744 | tf_op jit(solution)/shard_map/while/body/eval_jaxpr/all_gather | solution.py:22
  713.4 3.8 convolution_subtract_fusion.2
  717.3 62.1 %all-gather.10.cloned.1.call-done = f32[384,2048]{1,0:T(8,128)} async-done(((f32[48,2048]{1,0:T(8,128)}), f32[384,2048]{1,0:T(8,128)}) %all-gather.10.cloned.1.call-update) | async-done | bytes 3145744 | tf_op jit(solution)/shard_map/while/body/eval_jaxpr/all_gather | solution.py:22
  787.4 3.8 convolution_subtract_fusion.2
  791.3 62.1 %all-gather.10.cloned.1.call-done = f32[384,2048]{1,0:T(8,128)} async-done(((f32[48,2048]{1,0:T(8,128)}), f32[384,2048]{1,0:T(8,128)}) %all-gather.10.cloned.1.call-update) | async-done | bytes 3145744 | tf_op jit(solution)/shard_map/while/body/eval_jaxpr/all_gather | solution.py:22
  861.4 3.8 convolution_subtract_fusion.2
  865.3 62.1 %all-gather.10.cloned.1.call-done = f32[384,2048]{1,0:T(8,128)} async-done(((f32[48,2048]{1,0:T(8,128)}), f32[384,2048]{1,0:T(8,128)}) %all-gather.10.cloned.1.call-update) | async-done | bytes 3145744 | tf_op jit(solution)/shard_map/while/body/eval_jaxpr/all_gather | solution.py:22
  933.2 488.9 %while.33 = (s32[]{:T(128)}, f32[48,256]{1,0:T(8,128)S(1)}, f32[192,256]{1,0:T(8,128)S(1)}, s32[]{:T(128)}, f32[192,256]{1,0:T(8,128)S(1)}, /*index=5*/f32[256,2...) while((s32[]{:T(128)}, f32[48,256]{1,0:T(8,128)S(1)}, ...), condition=%wide.region_13.14_spmd, body=%wide.region_11.13_spmd.sunk | while | flops 604692480 | bytes 19628372 | solution.py:26
  940.1 59.7 %all-gather.12.cloned.1.call-done = f32[384,2048]{1,0:T(8,128)} async-done(((f32[48,2048]{1,0:T(8,128)}), f32[384,2048]{1,0:T(8,128)}) %all-gather.12.cloned.1.call-update) | async-done | bytes 3145744 | tf_op jit(solution)/shard_map/while/body/eval_jaxpr/all_gather | solution.py:22
  1010.0 59.7 %all-gather.12.cloned.1.call-done = f32[384,2048]{1,0:T(8,128)} async-done(((f32[48,2048]{1,0:T(8,128)}), f32[384,2048]{1,0:T(8,128)}) %all-gather.12.cloned.1.call-update) | async-done | bytes 3145744 | tf_op jit(solution)/shard_map/while/body/eval_jaxpr/all_gather | solution.py:22
  1079.8 59.7 %all-gather.12.cloned.1.call-done = f32[384,2048]{1,0:T(8,128)} async-done(((f32[48,2048]{1,0:T(8,128)}), f32[384,2048]{1,0:T(8,128)}) %all-gather.12.cloned.1.call-update) | async-done | bytes 3145744 | tf_op jit(solution)/shard_map/while/body/eval_jaxpr/all_gather | solution.py:22
  1149.6 59.7 %all-gather.12.cloned.1.call-done = f32[384,2048]{1,0:T(8,128)} async-done(((f32[48,2048]{1,0:T(8,128)}), f32[384,2048]{1,0:T(8,128)}) %all-gather.12.cloned.1.call-update) | async-done | bytes 3145744 | tf_op jit(solution)/shard_map/while/body/eval_jaxpr/all_gather | solution.py:22
  1219.5 59.7 %all-gather.12.cloned.1.call-done = f32[384,2048]{1,0:T(8,128)} async-done(((f32[48,2048]{1,0:T(8,128)}), f32[384,2048]{1,0:T(8,128)}) %all-gather.12.cloned.1.call-update) | async-done | bytes 3145744 | tf_op jit(solution)/shard_map/while/body/eval_jaxpr/all_gather | solution.py:22
  1289.3 59.7 %all-gather.12.cloned.1.call-done = f32[384,2048]{1,0:T(8,128)} async-done(((f32[48,2048]{1,0:T(8,128)}), f32[384,2048]{1,0:T(8,128)}) %all-gather.12.cloned.1.call-update) | async-done | bytes 3145744 | tf_op jit(solution)/shard_map/while/body/eval_jaxpr/all_gather | solution.py:22
  1359.2 59.7 %all-gather.12.cloned.1.call-done = f32[384,2048]{1,0:T(8,128)} async-done(((f32[48,2048]{1,0:T(8,128)}), f32[384,2048]{1,0:T(8,128)}) %all-gather.12.cloned.1.call-update) | async-done | bytes 3145744 | tf_op jit(solution)/shard_map/while/body/eval_jaxpr/all_gather | solution.py:22
  (147 shorter events, 138.6 us)
Async XLA Ops:
  175.5 70.0 %copy-start.5 = (f32[2048]{0:T(1024)S(1)}, f32[2048]{0:T(1024)}, u32[]{:S(2)}) copy-start(f32[2048]{0:T(1024)} %param.22) | copy-start | bytes 24580
  175.5 66.4 %all-to-all-start.1 = ((f32[4,24,256]{2,1,0:T(8,128)}), f32[4,24,256]{2,1,0:T(8,128)S(1)}, u32[]{:S(2)}, u32[]{:S(2)}) async-start(f32[4,24,256]{2,1,0:T(8,128)} %copy.20), calls=%async_computation.1 | async-start | bytes 196608 | tf_op jit(solution)/shard_map/all_to_all | solution.py:75
  242.0 165.3 %copy-start.6 = (f32[192]{0:T(256)}, f32[192]{0:T(256)S(1)}, u32[]{:S(2)}) copy-start(f32[192]{0:T(256)S(1)} %psum.7) | copy-start | bytes 2308
  242.0 7.8 all-to-all-start
  410.1 73.3 %all-gather.10.cloned.1.call-start = ((), (), s32[]{:S(2)}) async-start(), calls=%async_computation.2 | async-start | bytes 3538944 | tf_op jit(solution)/shard_map/while/body/eval_jaxpr/all_gather | solution.py:22
  410.1 6.4 collective-permute-start
  489.3 68.1 %all-gather.10.cloned.1.call-start = ((), (), s32[]{:S(2)}) async-start(), calls=%async_computation.2 | async-start | bytes 3538944 | tf_op jit(solution)/shard_map/while/body/eval_jaxpr/all_gather | solution.py:22
  489.3 2.2 collective-permute-start
  563.2 68.1 %all-gather.10.cloned.1.call-start = ((), (), s32[]{:S(2)}) async-start(), calls=%async_computation.2 | async-start | bytes 3538944 | tf_op jit(solution)/shard_map/while/body/eval_jaxpr/all_gather | solution.py:22
  563.3 2.2 collective-permute-start
  637.2 68.1 %all-gather.10.cloned.1.call-start = ((), (), s32[]{:S(2)}) async-start(), calls=%async_computation.2 | async-start | bytes 3538944 | tf_op jit(solution)/shard_map/while/body/eval_jaxpr/all_gather | solution.py:22
  637.3 2.2 collective-permute-start
  711.2 68.1 %all-gather.10.cloned.1.call-start = ((), (), s32[]{:S(2)}) async-start(), calls=%async_computation.2 | async-start | bytes 3538944 | tf_op jit(solution)/shard_map/while/body/eval_jaxpr/all_gather | solution.py:22
  711.3 2.2 collective-permute-start
  785.2 68.1 %all-gather.10.cloned.1.call-start = ((), (), s32[]{:S(2)}) async-start(), calls=%async_computation.2 | async-start | bytes 3538944 | tf_op jit(solution)/shard_map/while/body/eval_jaxpr/all_gather | solution.py:22
  785.3 2.2 collective-permute-start
  859.2 68.1 %all-gather.10.cloned.1.call-start = ((), (), s32[]{:S(2)}) async-start(), calls=%async_computation.2 | async-start | bytes 3538944 | tf_op jit(solution)/shard_map/while/body/eval_jaxpr/all_gather | solution.py:22
  859.2 2.2 collective-permute-start
  933.2 66.6 %all-gather.12.cloned.1.call-start = ((), (), s32[]{:S(2)}) async-start(), calls=%async_computation.3 | async-start | bytes 3538944 | tf_op jit(solution)/shard_map/while/body/eval_jaxpr/all_gather | solution.py:22
  933.3 3.1 collective-permute-start.1
  1003.1 66.6 %all-gather.12.cloned.1.call-start = ((), (), s32[]{:S(2)}) async-start(), calls=%async_computation.3 | async-start | bytes 3538944 | tf_op jit(solution)/shard_map/while/body/eval_jaxpr/all_gather | solution.py:22
  1003.1 3.1 collective-permute-start.1
  1072.9 66.6 %all-gather.12.cloned.1.call-start = ((), (), s32[]{:S(2)}) async-start(), calls=%async_computation.3 | async-start | bytes 3538944 | tf_op jit(solution)/shard_map/while/body/eval_jaxpr/all_gather | solution.py:22
  1073.0 3.1 collective-permute-start.1
  1142.8 66.6 %all-gather.12.cloned.1.call-start = ((), (), s32[]{:S(2)}) async-start(), calls=%async_computation.3 | async-start | bytes 3538944 | tf_op jit(solution)/shard_map/while/body/eval_jaxpr/all_gather | solution.py:22
  1142.8 3.1 collective-permute-start.1
  1212.6 66.6 %all-gather.12.cloned.1.call-start = ((), (), s32[]{:S(2)}) async-start(), calls=%async_computation.3 | async-start | bytes 3538944 | tf_op jit(solution)/shard_map/while/body/eval_jaxpr/all_gather | solution.py:22
  1212.7 3.1 collective-permute-start.1
  1282.4 66.6 %all-gather.12.cloned.1.call-start = ((), (), s32[]{:S(2)}) async-start(), calls=%async_computation.3 | async-start | bytes 3538944 | tf_op jit(solution)/shard_map/while/body/eval_jaxpr/all_gather | solution.py:22
  1282.5 3.1 collective-permute-start.1
  1352.3 66.6 %all-gather.12.cloned.1.call-start = ((), (), s32[]{:S(2)}) async-start(), calls=%async_computation.3 | async-start | bytes 3538944 | tf_op jit(solution)/shard_map/while/body/eval_jaxpr/all_gather | solution.py:22
  1352.3 3.1 collective-permute-start.1
  (6 other events, 171.2 us)
Sparse Core Ops, SparseCore 0:
  420.5 62.8 all-gather.9
  495.4 61.9 all-gather.9
  569.4 61.9 all-gather.9
  643.4 61.9 all-gather.9
  717.4 61.9 all-gather.9
  791.4 61.9 all-gather.9
  865.4 61.9 all-gather.9
  940.2 59.5 all-gather.11
  1010.1 59.5 all-gather.11
  1079.9 59.5 all-gather.11
  1149.8 59.5 all-gather.11
  1219.6 59.5 all-gather.11
  1289.4 59.5 all-gather.11
  1359.3 59.5 all-gather.11
